TPU v7x, 32 devices: a whole 2x2x4 slice. The times are simulated.
32 devices in a mesh: dp: 4 (over y, x), expert: 4 (over z), tok: 2 (over core).
Axes of the slice: x: 2, y: 2, z: 4, core: 2. Of those that a mesh axis runs over, the one named last changes fastest.
Arguments:
- tokens: bfloat16 [32768, 512], P(('dp', 'expert', 'tok')), may hold values from -6 to 6
- out_grad: bfloat16 [32768, 512], P(('dp', 'expert', 'tok')), may hold values from -6 to 6
- expert_ids: int32 [32768, 2], P(('dp', 'expert', 'tok')), may hold values from 0 to 3, all different within a row; in each aligned block of 1024 rows (0 to 1023, 1024 to 2047, ...) at most 768 rows name the same one
- sentence_ids: int32 [32, 1024], P(('dp', 'expert', 'tok')), may hold values from 0 to 15, never falling along the last dimension, each value on 1 to 128 neighbouring positions
- ln_attn: float32 [512], replicated, may hold values from 0.25 to 1.75
- w_kv: bfloat16 [512, 128], replicated, may hold values from -0.25 to 0.25
- w_router: bfloat16 [512, 4], replicated, may hold values from -0.1875 to 0.1875
- w_query: bfloat16 [4, 512, 64], P('expert'), may hold values from -0.25 to 0.25
- w_output: bfloat16 [4, 64, 512], P('expert'), may hold values from -4 to 4
- ln_ffn: float32 [512], replicated, may hold values from 0.25 to 1.75
- w_in: bfloat16 [512, 2048], replicated, may hold values from -0.25 to 0.25
- w_out: bfloat16 [2048, 512], replicated, may hold values from -0.1875 to 0.1875
Outputs:
- output: bfloat16 [32768, 512], P(('dp', 'expert', 'tok'))
- grad_tokens: bfloat16 [32768, 512], P(('dp', 'expert', 'tok'))
- grad_ln_attn: float32 [512], replicated
- grad_kv: float32 [512, 128], replicated
- grad_router: float32 [512, 4], replicated
- grad_query: float32 [4, 512, 64], P('expert')
- grad_output: float32 [4, 64, 512], P('expert')
- grad_ln_ffn: float32 [512], replicated
- grad_in: float32 [512, 2048], replicated
- grad_out: float32 [2048, 512], replicated
Inputs may be any that keep to these rules, and one draw needn't show every extreme that they name: `expert_ids`: among the 1024 rows of one device no expert is named more than 768 times, a bound that some block reaches; a token's 2 ids differ. `sentence_ids`: in each device's row the ids never fall; each id covers 1 to 128 consecutive positions, one exactly 128.
All inputs are finite; a program needn't handle non-finite values.
Results may differ from a plain program's by a relative error of at most 0.017.
Values may be sent and summed in bfloat16 or wider, within the bound.
No kernel may reach another device: no remote copies, remote signals or barrier semaphores. Data moves between devices by JAX's collectives and lax.ppermute only.
A program may use at most 128 MiB of HBM per device.

v0:
```python
import jax
import jax.numpy as jnp
from jax import lax
from jax.sharding import PartitionSpec as P


def product(left, right):
    return jnp.dot(left, right, preferred_element_type=jnp.float32)


def product_tn(left, right):
    return lax.dot_general(
        left, right, (((0,), (0,)), ((), ())), preferred_element_type=jnp.float32
    )


def product_nt(left, right):
    return lax.dot_general(
        left, right, (((1,), (1,)), ((), ())), preferred_element_type=jnp.float32
    )


def layer_norm_parts(values, gain):
    centre = values - jnp.mean(values, axis=-1, keepdims=True)
    spread = jnp.mean(centre * centre, axis=-1, keepdims=True)
    inverse = lax.rsqrt(spread + 1e-05)
    normalized = centre * inverse
    return (normalized * gain, normalized, inverse)


def layer_norm_back(upstream, normalized, inverse, gain):
    scaled = upstream * gain
    gain_grad = jnp.sum(upstream * normalized, axis=0)
    inner = (
        scaled
        - jnp.mean(scaled, axis=-1, keepdims=True)
        - normalized * jnp.mean(scaled * normalized, axis=-1, keepdims=True)
    )
    return (inner * inverse, gain_grad)


def gelu_exact(values):
    return 0.5 * values * (1.0 + jax.scipy.special.erf(values * 0.7071067811865476))


def gelu_slope(values):
    cumulative = 0.5 * (1.0 + jax.scipy.special.erf(values * 0.7071067811865476))
    density = jnp.exp(-0.5 * values * values) * 0.3989422804014327
    return cumulative + values * density


def head_forward(rows, row_ids, shared, key_ids, query_weight, output_weight):
    head_size = query_weight.shape[1]
    queries = product(rows, query_weight).astype(jnp.bfloat16)
    scores = product_nt(queries, shared[:, :head_size]) * 0.125
    scores = jnp.where(row_ids[:, None] == key_ids[None, :], scores, -30000.0)
    largest = jnp.max(scores, axis=-1, keepdims=True)
    raised = jnp.exp(scores - largest)
    total = jnp.sum(raised, axis=-1, keepdims=True)
    weights = (raised / total).astype(jnp.bfloat16)
    attended = product(weights, shared[:, head_size:]).astype(jnp.bfloat16)
    result = product(attended, output_weight).astype(jnp.bfloat16)
    log_total = largest[:, 0] + jnp.log(total[:, 0])
    return (result, queries, attended, log_total)


def head_backward(
    rows,
    row_ids,
    shared,
    key_ids,
    query_weight,
    output_weight,
    queries,
    attended,
    log_total,
    result_grad,
):
    head_size = query_weight.shape[1]
    output_grad = product_tn(attended, result_grad)
    attended_grad = product_nt(result_grad, output_weight).astype(jnp.bfloat16)
    scores = product_nt(queries, shared[:, :head_size]) * 0.125
    scores = jnp.where(row_ids[:, None] == key_ids[None, :], scores, -30000.0)
    probs = jnp.exp(scores - log_total[:, None])
    prob_low = probs.astype(jnp.bfloat16)
    prob_grad = product_nt(attended_grad, shared[:, head_size:])
    score_grad = (probs * (prob_grad - jnp.sum(probs * prob_grad, axis=-1, keepdims=True))).astype(
        jnp.bfloat16
    )
    query_grad = (product(score_grad, shared[:, :head_size]) * 0.125).astype(jnp.bfloat16)
    key_grad = product_tn(score_grad, queries) * 0.125
    value_grad = product_tn(prob_low, attended_grad)
    shared_grad = jnp.concatenate([key_grad, value_grad], axis=1)
    query_weight_grad = product_tn(rows, query_grad)
    rows_grad = product_nt(query_grad, query_weight).astype(jnp.bfloat16)
    return (rows_grad, shared_grad, query_weight_grad, output_grad)


def body(
    tokens,
    out_grad,
    expert_ids,
    sentence_ids,
    ln_attn,
    w_kv,
    w_router,
    w_query,
    w_output,
    ln_ffn,
    w_in,
    w_out,
):
    length = tokens.shape[0]
    width = tokens.shape[1]
    choose = expert_ids.shape[1]
    head_size = w_query.shape[2]
    experts = lax.axis_size("expert")
    capacity = 3 * length // experts
    sentence = sentence_ids[0]
    inputs = tokens.astype(jnp.float32)
    normed, norm_one, inverse_one = layer_norm_parts(inputs, ln_attn)
    normed_low = normed.astype(jnp.bfloat16)
    shared = product(normed_low, w_kv).astype(jnp.bfloat16)
    logits = product(normed_low, w_router)
    expert_range = jnp.arange(experts, dtype=jnp.int32)
    selector = (expert_ids[:, :, None] == expert_range[None, None, :]).astype(jnp.float32)
    picked = jnp.sum(selector * logits[:, None, :], axis=2)
    picked_top = jnp.max(picked, axis=-1, keepdims=True)
    picked_raised = jnp.exp(picked - picked_top)
    gates = picked_raised / jnp.sum(picked_raised, axis=-1, keepdims=True)
    flat_expert = expert_ids.reshape(length * choose)
    member = (flat_expert[:, None] == expert_range[None, :]).astype(jnp.int32)
    earlier = jnp.cumsum(member, axis=0) - member
    position = jnp.sum(earlier * member, axis=1)
    slot_index = flat_expert * capacity + position
    routed_rows = jnp.broadcast_to(normed_low[:, None, :], (length, choose, width)).reshape(
        length * choose, width
    )
    routed_ids = jnp.broadcast_to(sentence[:, None], (length, choose)).reshape(length * choose)
    dispatch_rows = (
        jnp.zeros((experts * capacity, width), jnp.bfloat16)
        .at[slot_index]
        .set(routed_rows)
        .reshape(experts, capacity, width)
    )
    dispatch_ids = (
        jnp.full((experts * capacity,), -1, jnp.int32)
        .at[slot_index]
        .set(routed_ids)
        .reshape(experts, capacity)
    )
    arrived, arrived_ids = (
        lax.all_to_all(dispatch_rows, "expert", split_axis=0, concat_axis=0, tiled=True),
        lax.all_to_all(dispatch_ids, "expert", split_axis=0, concat_axis=0, tiled=True),
    )
    all_shared, all_ids = (
        lax.all_gather(shared, "expert", axis=0, tiled=True),
        lax.all_gather(sentence, "expert", axis=0, tiled=True),
    )
    all_shared = all_shared.reshape(experts, length, 2 * head_size)
    all_ids = all_ids.reshape(experts, length)
    own_query = w_query[0]
    own_output = w_output[0]

    def forward_item(item):
        rows, row_ids, item_shared, key_ids = item
        return head_forward(rows, row_ids, item_shared, key_ids, own_query, own_output)

    results, kept_queries, kept_attended, kept_totals = lax.map(
        forward_item, (arrived, arrived_ids, all_shared, all_ids)
    )
    returned = lax.all_to_all(results, "expert", split_axis=0, concat_axis=0, tiled=True)
    returned_rows = (
        returned.reshape(experts * capacity, width)[slot_index]
        .astype(jnp.float32)
        .reshape(length, choose, width)
    )
    mixed = jnp.sum(gates[:, :, None] * returned_rows, axis=1)
    hidden_in = inputs + mixed
    normed_two, norm_two, inverse_two = layer_norm_parts(hidden_in, ln_ffn)
    normed_two_low = normed_two.astype(jnp.bfloat16)
    before = product(normed_two_low, w_in)
    activated = gelu_exact(before).astype(jnp.bfloat16)
    output = (hidden_in + product(activated, w_out)).astype(jnp.bfloat16)
    out_weight_grad = product_tn(activated, out_grad)
    activated_grad = product_nt(out_grad, w_out)
    before_grad = (activated_grad * gelu_slope(before)).astype(jnp.bfloat16)
    in_weight_grad = product_tn(normed_two_low, before_grad)
    normed_two_grad = product_nt(before_grad, w_in)
    hidden_back, ln_ffn_grad = layer_norm_back(normed_two_grad, norm_two, inverse_two, ln_ffn)
    hidden_grad = out_grad.astype(jnp.float32) + hidden_back
    gate_grad = jnp.sum(hidden_grad[:, None, :] * returned_rows, axis=2)
    picked_grad = gates * (gate_grad - jnp.sum(gates * gate_grad, axis=-1, keepdims=True))
    logits_grad = jnp.sum(selector * picked_grad[:, :, None], axis=1).astype(jnp.bfloat16)
    router_grad = product_tn(normed_low, logits_grad)
    route_grad = (
        (gates[:, :, None] * hidden_grad[:, None, :])
        .astype(jnp.bfloat16)
        .reshape(length * choose, width)
    )
    route_dispatch = (
        jnp.zeros((experts * capacity, width), jnp.bfloat16)
        .at[slot_index]
        .set(route_grad)
        .reshape(experts, capacity, width)
    )
    arrived_grad = lax.all_to_all(route_dispatch, "expert", split_axis=0, concat_axis=0, tiled=True)

    def backward_item(item):
        rows, row_ids, item_shared, key_ids, queries, attended, totals, result_grad = item
        return head_backward(
            rows,
            row_ids,
            item_shared,
            key_ids,
            own_query,
            own_output,
            queries,
            attended,
            totals,
            result_grad,
        )

    rows_grad, shared_parts, query_parts, output_parts = lax.map(
        backward_item,
        (
            arrived,
            arrived_ids,
            all_shared,
            all_ids,
            kept_queries,
            kept_attended,
            kept_totals,
            arrived_grad,
        ),
    )
    back_rows = lax.all_to_all(rows_grad, "expert", split_axis=0, concat_axis=0, tiled=True)
    shared_grad = lax.psum_scatter(
        shared_parts.reshape(experts * length, 2 * head_size).astype(jnp.bfloat16),
        "expert",
        scatter_dimension=0,
        tiled=True,
    )
    query_grad_sum = jnp.sum(query_parts, axis=0)[None]
    output_grad_sum = jnp.sum(output_parts, axis=0)[None]
    query_total, output_total = (
        lax.psum(query_grad_sum.astype(jnp.bfloat16), ("dp", "tok")).astype(jnp.float32),
        lax.psum(output_grad_sum.astype(jnp.bfloat16), ("dp", "tok")).astype(jnp.float32),
    )
    kv_weight_grad = product_tn(normed_low, shared_grad)
    routes_back = (
        back_rows.reshape(experts * capacity, width)[slot_index]
        .astype(jnp.float32)
        .reshape(length, choose, width)
    )
    normed_grad = (
        product_nt(shared_grad, w_kv)
        + product_nt(logits_grad, w_router)
        + jnp.sum(routes_back, axis=1)
    )
    input_back, ln_attn_grad = layer_norm_back(normed_grad, norm_one, inverse_one, ln_attn)
    input_grad = (hidden_grad + input_back).astype(jnp.bfloat16)
    summed = lax.psum(
        (ln_attn_grad, kv_weight_grad, router_grad, in_weight_grad, out_weight_grad, ln_ffn_grad),
        ("dp", "expert", "tok"),
    )
    return (
        output,
        input_grad,
        summed[0],
        summed[1],
        summed[2],
        query_total,
        output_total,
        summed[5],
        summed[3],
        summed[4],
    )


def solution(mesh):
    return jax.shard_map(
        body,
        mesh=mesh,
        in_specs=(
            P(("dp", "expert", "tok"), None),
            P(("dp", "expert", "tok"), None),
            P(("dp", "expert", "tok"), None),
            P(("dp", "expert", "tok"), None),
            P(),
            P(),
            P(),
            P("expert", None, None),
            P("expert", None, None),
            P(),
            P(),
            P(),
        ),
        out_specs=(
            P(("dp", "expert", "tok"), None),
            P(("dp", "expert", "tok"), None),
            P(),
            P(),
            P(),
            P("expert", None, None),
            P("expert", None, None),
            P(),
            P(),
            P(),
        ),
        check_vma=False,
    )
```

profile of v0, /device:TPU:0, one launch (start us, length us, event | category | flops | bytes accessed | tf_op | source)
XLA Modules:
  0.0 818.5 jit_solution(17089918963078222424)
XLA Ops:
  19.5 8.6 %scatter_custom_fusion = s32[3072]{0:T(1024)} fusion(s32[2048]{0:T(1024)S(1)} %bitcast.203, s32[2048]{0:T(1024)S(1)} %reshape.331, s32[]{:T(128)} %constant.101.clone.1), kind=kCustom, calls=%fused_computation.137 | custom fusion | bytes 12292 | tf_op jit(solution)/shard_map/scatter | solution.py:149
  28.2 6.3 all-to-all-start
  40.0 4.1 reshape.339
  44.1 12.1 %scatter_custom_fusion.1 = bf16[3072,512]{1,0:T(8,128)(2,1)} fusion(s32[2048]{0:T(1024)S(1)} %bitcast.204, bf16[2048,512]{1,0:T(8,128)(2,1)} %reshape.339, bf16[]{:T(256)} %constant.98.clone.1), kind=kCustom, calls=%fused_computation.115 | custom fusion | bytes 3146240 | tf_op jit(solution)/shard_map/scatter | solution.py:143
  56.1 5.2 all-to-all-start.1
  62.6 91.3 %all-gather = s32[1,4096]{1,0:T(1,128)S(1)} all-gather(s32[1,1024]{1,0:T(1,128)S(1)} %copy-done.35), channel_id=2, replica_groups=mesh['dp'=4,'expert'=4,'tok'=2] {'expert'}, dimensions={1}, use_global_device_ids=true | all-gather | bytes 20480 | tf_op jit(solution)/shard_map/all_gather | solution.py:158
  157.8 41.3 %while.32 = (s32[]{:T(128)}, bf16[4,768,512]{2,1,0:T(8,128)(2,1)}, bf16[4,768,64]{1,2,0:T(8,128)(2,1)}, bf16[4,768,64]{1,2,0:T(8,128)(2,1)}, f32[4,768]{1,0:T(4,...) while((s32[]{:T(128)}, bf16[4,768,512]{2,1,0:T(8,128)(2,1)}, ...), condition=%wide.region_13.14_spmd, body=%wide.region_10.13_spmd.sunk | while | flops 314277120 | bytes 12918941 | solution.py:169
  199.1 4.8 all-to-all-start.2
  204.9 66.7 %all-to-all-done.2 = bf16[4,768,512]{2,1,0:T(8,128)(2,1)} async-done(((bf16[4,768,512]{2,1,0:T(8,128)(2,1)}), bf16[4,768,512]{2,1,0:T(8,128)(2,1)}, u32[]{:S(2)}, u32[]{:S(2)}) %all-to-all-start.2) | async-done | bytes 3145760 | tf_op jit(solution)/shard_map/all_to_all | solution.py:172
  271.6 11.6 %gather_fusion = bf16[2048,512]{1,0:T(8,128)(2,1)} fusion(bf16[3072,512]{1,0:T(8,128)(2,1)} %bitcast.25, s32[2048]{0:T(1024)S(1)} %broadcast_clamp_fusion), kind=kCustom, calls=%fused_computation | custom fusion | bytes 4202496 | tf_op jit(solution)/shard_map/gather | solution.py:174
  283.2 5.4 reshape.309
  288.6 7.7 multiply_reduce_fusion.2
  297.1 4.7 multiply_convert_fusion.1
  301.8 5.0 fusion.47
  316.2 6.2 mul.257
  322.5 13.1 %scatter_custom_fusion.2 = bf16[3072,512]{1,0:T(8,128)(2,1)} fusion(s32[2048]{0:T(1024)S(1)} %bitcast.206, f32[2048,512]{1,0:T(8,128)} %mul.257, f32[2048]{0:T(1024)S(1)} %div.59, bf16[]{:T(256)} %constant.98.clone.1), kind=kCustom, calls=%fused_computation.102 | custom fusion | flops 2097152 | bytes 7348226 | tf_op jit(solution)/shard_map/scatter | solution.py:204
  339.4 70.0 %all-to-all-done.3 = bf16[4,768,512]{2,1,0:T(8,128)(2,1)S(1)} async-done(((bf16[4,768,512]{2,1,0:T(8,128)(2,1)}), bf16[4,768,512]{2,1,0:T(8,128)(2,1)S(1)}, u32[]{:S(2)}, u32[]{:S(2)}) %all-to-all-start.3) | async-done | bytes 3145760 | tf_op jit(solution)/shard_map/all_to_all | solution.py:207
  411.3 68.2 %while.33 = (s32[]{:T(128)}, bf16[4,768,512]{2,1,0:T(8,128)(2,1)}, bf16[4,1024,128]{2,1,0:T(8,128)(2,1)}, f32[4,512,64]{1,2,0:T(8,128)}, f32[4,64,512]{2,1,0:T(8...) while((s32[]{:T(128)}, bf16[4,768,512]{2,1,0:T(8,128)(2,1)}, ...), condition=%wide.region_22.23_spmd, body=%wide.region_20.22_spmd.sunk | while | flops 713702656 | bytes 31267520 | solution.py:224
  479.6 3.7 all-to-all-start.4
  483.8 7.2 fusion.84
  491.0 4.6 fusion.78
  499.1 30.9 %reduce-scatter.2.cloned.1.call-done = bf16[1024,128]{1,0:T(8,128)(2,1)} async-done(((bf16[4096,128]{1,0:T(8,128)(2,1)}), bf16[1024,128]{1,0:T(8,128)(2,1)}) %reduce-scatter.2.cloned.1.call-update) | async-done | bytes 262160 | tf_op jit(solution)/shard_map/reduce_scatter | solution.py:238
  532.5 5.9 multiply_reduce_fusion.1
  541.8 6.8 add_convert_fusion
  548.6 64.8 %all-reduce.8.cloned.1.call-done = (bf16[1,512,64]{1,2,0:T(8,128)(2,1)}, bf16[1,64,512]{2,1,0:T(8,128)(2,1)}) async-done(((bf16[1,512,64]{1,2,0:T(8,128)(2,1)}, bf16[1,64,512]{2,1,0:T(8,128)(2,1)}), (bf16[1,512,64]{1,2,0:T(8,128)(2,1)}, bf16[1,64,512]{2,1,0:T(8,128)(2,1)})) %all-reduce.8.cloned.1.call-update) | async-done | bytes 131088 | tf_op jit(solution)/shard_map/psum | solution.py:247
  618.2 9.4 %gather_fusion.1 = bf16[2048,512]{1,0:T(8,128)(2,1)} fusion(bf16[3072,512]{1,0:T(8,128)(2,1)S(1)} %bitcast.191, s32[2048]{0:T(1024)S(1)} %copy-done.22), kind=kCustom, calls=%fused_computation.1 | custom fusion | bytes 4202496 | tf_op jit(solution)/shard_map/gather | solution.py:252
  627.6 5.5 reshape.310
  633.1 8.7 %reduce_sum.214 = f32[1024,512]{1,0:T(8,128)} reduce(f32[1024,2,512]{2,1,0:T(2,128)} %reshape.310, f32[]{:T(128)} %constant.71.clone.1), dimensions={1}, to_apply=%region_27.28 | reduce | flops 524288 | bytes 6291460 | tf_op jit(solution)/shard_map/reduce_sum | solution.py:259
  641.9 4.8 fusion.60
  646.7 40.1 %all-reduce = (f32[512]{0:T(512)}, f32[512,4]{0,1:T(4,128)}, f32[512]{0:T(512)}) all-reduce(f32[512]{0:T(512)S(1)} %get-tuple-element.235, f32[512,4]{0,1:T(4,128)S(1)} %copy-done.28, f32[512]{0:T(512)S(1)} %copy-done.36), channel_id=1, replica_groups=mesh['dp'=4,'expert'=4,'tok'=2] {'dp','expert','tok'}, use_global_device_ids=true, to_apply=%region_31.32 | all-reduce | flops 3072 | bytes 24576 | tf_op jit(solution)/shard_map/psum | solution.py:263
  689.9 113.4 %all-reduce.6.cloned.1.call-done = (f32[512,128]{1,0:T(8,128)}, f32[512,2048]{1,0:T(8,128)}, f32[2048,512]{1,0:T(8,128)}) async-done(((f32[512,128]{1,0:T(8,128)}, f32[512,2048]{1,0:T(8,128)}, f32[2048,512]{1,0:T(8,128)}), (f32[512,128]{1,0:T(8,128)}, f32[512,2048]{1,0:T(8,128)}, f32[2048,512]{1,0:T(8,128)})) %all-reduce.6.cloned.1.call-update) | async-done | bytes 8650768 | tf_op jit(solution)/shard_map/psum | solution.py:263
  805.0 4.8 copy.166
  (268 shorter events, 170.1 us)
Async XLA Ops:
  7.2 289.8 %copy-start = (bf16[512,2048]{1,0:T(8,128)(2,1)S(1)}, bf16[512,2048]{1,0:T(8,128)(2,1)}, u32[]{:S(2)}) copy-start(bf16[512,2048]{1,0:T(8,128)(2,1)} %param.26) | copy-start | bytes 6291460
  7.2 27.3 %copy-start.5 = (bf16[1024,512]{1,0:T(8,128)(2,1)S(1)}, bf16[1024,512]{1,0:T(8,128)(2,1)}, u32[]{:S(2)}) copy-start(bf16[1024,512]{1,0:T(8,128)(2,1)} %param.16) | copy-start | bytes 3145732
  7.2 28.7 %copy-start.29 = (f32[512]{0:T(512)S(1)}, f32[512]{0:T(512)}, u32[]{:S(2)}) copy-start(f32[512]{0:T(512)} %param.20) | copy-start | bytes 6148
  28.2 28.0 %all-to-all-start = ((s32[4,1,768]{2,1,0:T(1,128)}), s32[4,1,768]{2,1,0:T(1,128)S(1)}, u32[]{:S(2)}, u32[]{:S(2)}) async-start(s32[4,1,768]{2,1,0:T(1,128)} %bitcast.20), calls=%async_computation | async-start | bytes 24576 | tf_op jit(solution)/shard_map/all_to_all | solution.py:154
  37.5 166.3 %copy-start.4 = (bf16[1024,512]{1,0:T(8,128)(2,1)}, bf16[1024,512]{1,0:T(8,128)(2,1)S(1)}, u32[]{:S(2)}) copy-start(bf16[1024,512]{1,0:T(8,128)(2,1)S(1)} %fusion.54) | copy-start | bytes 3145732
  56.1 99.0 %copy-start.25 = (bf16[1,512,64]{1,2,0:T(8,128)(2,1)S(1)}, bf16[1,512,64]{1,2,0:T(8,128)(2,1)}, u32[]{:S(2)}) copy-start(bf16[1,512,64]{1,2,0:T(8,128)(2,1)} %param.23) | copy-start | bytes 196612
  56.1 99.7 %all-to-all-start.1 = ((bf16[4,768,512]{2,1,0:T(8,128)(2,1)}), bf16[4,768,512]{2,1,0:T(8,128)(2,1)}, u32[]{:S(2)}, u32[]{:S(2)}) async-start(bf16[4,768,512]{2,1,0:T(8,128)(2,1)} %bitcast.192), calls=%async_computation.1 | async-start | bytes 6291456 | tf_op jit(solution)/shard_map/all_to_all | solution.py:153
  61.4 94.5 %all-gather.3.cloned.1.call-start = ((), (), s32[]{:S(2)}) async-start(), calls=%async_computation.6 | async-start | bytes 1310720 | tf_op jit(solution)/shard_map/all_gather | solution.py:157
  199.1 72.5 %all-to-all-start.2 = ((bf16[4,768,512]{2,1,0:T(8,128)(2,1)}), bf16[4,768,512]{2,1,0:T(8,128)(2,1)}, u32[]{:S(2)}, u32[]{:S(2)}) async-start(bf16[4,768,512]{2,1,0:T(8,128)(2,1)} %get-tuple-element.150), calls=%async_computation.2 | async-start | bytes 6291456 | tf_op jit(solution)/shard_map/all_to_all | solution.py:172
  204.4 78.8 %copy-start.26 = (f32[1024]{0:T(1024)}, f32[1024]{0:T(1024)S(1)}, u32[]{:S(2)}) copy-start(f32[1024]{0:T(1024)S(1)} %fusion.74) | copy-start | bytes 12292
  204.9 78.2 %copy-start.21 = (s32[2048]{0:T(1024)}, s32[2048]{0:T(1024)S(1)}, u32[]{:S(2)}) copy-start(s32[2048]{0:T(1024)S(1)} %broadcast_clamp_fusion) | copy-start | bytes 24580
  288.6 7.7 copy-start.6
  296.6 13.7 %copy-start.2 = (f32[1024,512]{1,0:T(8,128)}, f32[1024,512]{1,0:T(8,128)S(1)}, u32[]{:S(2)}) copy-start(f32[1024,512]{1,0:T(8,128)S(1)} %get-tuple-element.300) | copy-start | bytes 6291460
  335.6 73.8 %all-to-all-start.3 = ((bf16[4,768,512]{2,1,0:T(8,128)(2,1)}), bf16[4,768,512]{2,1,0:T(8,128)(2,1)S(1)}, u32[]{:S(2)}, u32[]{:S(2)}) async-start(bf16[4,768,512]{2,1,0:T(8,128)(2,1)} %bitcast.193), calls=%async_computation.3 | async-start | bytes 6291456 | tf_op jit(solution)/shard_map/all_to_all | solution.py:207
  339.3 190.7 %reduce-scatter.2.cloned.1.call-start = ((), (), s32[]{:S(2)}) async-start(), calls=%async_computation.7 | async-start | bytes 1310720 | tf_op jit(solution)/shard_map/reduce_scatter | solution.py:238
  479.6 138.6 %all-to-all-start.4 = ((bf16[4,768,512]{2,1,0:T(8,128)(2,1)}), bf16[4,768,512]{2,1,0:T(8,128)(2,1)S(1)}, u32[]{:S(2)}, u32[]{:S(2)}) async-start(bf16[4,768,512]{2,1,0:T(8,128)(2,1)} %get-tuple-element.155), calls=%async_computation.5 | async-start | bytes 6291456 | tf_op jit(solution)/shard_map/all_to_all | solution.py:237
  483.3 130.1 %all-reduce.8.cloned.1.call-start = ((), (), s32[]{:S(2)}) async-start(), calls=%async_computation.9 | async-start | bytes 262144 | tf_op jit(solution)/shard_map/psum | solution.py:247
  483.8 7.2 copy-start.3
  483.8 7.2 copy-start.11
  483.8 7.2 copy-start.32
  499.0 304.3 %all-reduce.6.cloned.1.call-start = ((), (), s32[]{:S(2)}) async-start(), calls=%async_computation.8 | async-start | bytes 17301504 | tf_op jit(solution)/shard_map/psum | solution.py:263
  532.4 7.2 copy-start.27
  532.4 7.2 copy-start.18
  541.8 74.6 %copy-start.13 = (bf16[1024,128]{1,0:T(8,128)(2,1)S(1)}, bf16[1024,128]{1,0:T(8,128)(2,1)}, u32[]{:S(2)}) copy-start(bf16[1024,128]{1,0:T(8,128)(2,1)} %reduce-scatter.2.cloned.1.call-done) | copy-start | bytes 786436
  541.8 74.6 %copy-start.16 = (bf16[512,128]{1,0:T(8,128)(2,1)S(1)}, bf16[512,128]{1,0:T(8,128)(2,1)}, u32[]{:S(2)}) copy-start(bf16[512,128]{1,0:T(8,128)(2,1)} %param.21) | copy-start | bytes 393220
  541.8 76.4 %copy-start.22 = (s32[2048]{0:T(1024)S(1)}, s32[2048]{0:T(1024)}, u32[]{:S(2)}) copy-start(s32[2048]{0:T(1024)} %copy-done.21) | copy-start | bytes 24580
  633.1 8.7 %copy-start.7 = (bf16[1024,512]{1,0:T(8,128)(2,1)S(1)}, bf16[1024,512]{1,0:T(8,128)(2,1)}, u32[]{:S(2)}) copy-start(bf16[1024,512]{1,0:T(8,128)(2,1)} %param.16) | copy-start | bytes 3145732
  633.1 8.7 %copy-start.20 = (f32[1024]{0:T(1024)S(1)}, f32[1024]{0:T(1024)}, u32[]{:S(2)}) copy-start(f32[1024]{0:T(1024)} %copy-done.19) | copy-start | bytes 12292
  633.1 8.7 %copy-start.24 = (f32[1024]{0:T(1024)S(1)}, f32[1024]{0:T(1024)}, u32[]{:S(2)}) copy-start(f32[1024]{0:T(1024)} %copy-done.23) | copy-start | bytes 12292
  633.1 8.7 %copy-start.30 = (f32[512]{0:T(512)S(1)}, f32[512]{0:T(512)}, u32[]{:S(2)}) copy-start(f32[512]{0:T(512)} %param.20) | copy-start | bytes 6148
  633.1 8.7 %copy-start.34 = (bf16[512,4]{0,1:T(4,128)(2,1)S(1)}, bf16[512,4]{0,1:T(4,128)(2,1)}, u32[]{:S(2)}) copy-start(bf16[512,4]{0,1:T(4,128)(2,1)} %param.22) | copy-start | bytes 12292
  641.9 45.0 %copy-start.9 = (f32[1024,512]{1,0:T(8,128)S(1)}, f32[1024,512]{1,0:T(8,128)}, u32[]{:S(2)}) copy-start(f32[1024,512]{1,0:T(8,128)} %copy-done.8) | copy-start | bytes 6291460
  (15 other events, 59.3 us)
Sparse Core Ops, SparseCore 0:
  64.3 43.4 all-gather.2
  479.7 50.2 reduce-scatter.1
  533.9 79.4 all-reduce.7
  620.0 183.2 all-reduce.5
where the time goes:
time: 829 us; the launch traced here: 819 us
  waiting for transfers between devices  346 us (42%)
  blocking collectives  131 us (16%)
  matrix products  122 us (15%)
  local copies, waits for them, and re-layouts  120 us (14%)
  other arithmetic  60.4 us (7%)
  starting transfers between devices  24.3 us (3%)
  between operations  14.5 us (2%)
    psum x1, waiting for transfers between devices, body(): lax.psum((ln_attn_grad, kv_weight_grad, router_grad, in_weight_grad, out_...  113 us
    all_gather x1, blocking collectives, body(): lax.all_gather(sentence, 'expert', axis=0, tiled=True)  91.3 us
    all_to_all x1, waiting for transfers between devices, body(): lax.all_to_all(route_dispatch, 'expert', split_axis=0, concat_axis=0, til...  70 us
    all_to_all x1, waiting for transfers between devices, body(): lax.all_to_all(results, 'expert', split_axis=0, concat_axis=0, tiled=True)  66.7 us
    psum x1, waiting for transfers between devices, body(): lax.psum(query_grad_sum.astype(jnp.bfloat16), ('dp', 'tok'))  64.8 us
    dot_general x24, matrix products, product_nt(): lax.dot_general(left, right, (((1,), (1,)), ((), ())), preferred_element_...  43.4 us
    dot_general x20, matrix products, product(): return jnp.dot(left, right, preferred_element_type=jnp.float32)  40.2 us
    psum x1, blocking collectives, body(): lax.psum((ln_attn_grad, kv_weight_grad, router_grad, in_weight_grad, out_...  40.1 us
  transfers between devices with their start and end apart: 9, of which 5 were waited for; matrix products, arithmetic and copies ran while one was open for 12% of the time, Pallas kernels for 0%

commit v1 on v0

--- a/solution.py
+++ b/solution.py
@@ -261,8 +261,18 @@
     input_back, ln_attn_grad = layer_norm_back(normed_grad, norm_one, inverse_one, ln_attn)
     input_grad = (hidden_grad + input_back).astype(jnp.bfloat16)
     summed = lax.psum(
-        (ln_attn_grad, kv_weight_grad, router_grad, in_weight_grad, out_weight_grad, ln_ffn_grad),
-        ("dp", "expert", "tok"),
+        lax.psum(
+            (
+                ln_attn_grad,
+                kv_weight_grad,
+                router_grad,
+                in_weight_grad,
+                out_weight_grad,
+                ln_ffn_grad,
+            ),
+            ("expert", "tok"),
+        ),
+        "dp",
     )
     return (
         output,

time: 829 us -> 953 us (1.15)
  waiting for transfers between devices: 346 us -> 468 us
    psum x0 -> x1, waiting for transfers between devices: none -> 88.3 us  [body(): lax.psum(lax.psum((ln_attn_grad, kv_weight_grad, router_grad, in_weight_g...]
    psum x1, waiting for transfers between devices: 113 us -> 179 us  [body(): lax.psum((ln_attn_grad, kv_weight_grad, router_grad, in_weight_grad, out_...]
    psum x1, waiting for transfers between devices: 64.8 us -> 37 us  [body(): lax.psum(query_grad_sum.astype(jnp.bfloat16), ('dp', 'tok'))]
    psum x0 -> x1, blocking collectives: none -> 17.2 us  [body(): lax.psum(lax.psum((ln_attn_grad, kv_weight_grad, router_grad, in_weight_g...]
    reduce_scatter x1, waiting for transfers between devices: 30.9 us -> 14.3 us  [body(): lax.psum_scatter(shared_parts.reshape(experts * length, 2 * head_size).as...]
    psum x1, blocking collectives: 40.1 us -> 26.2 us  [body(): lax.psum((ln_attn_grad, kv_weight_grad, router_grad, in_weight_grad, out_...]
    all_to_all x1, waiting for transfers between devices: 0.01 us -> 12.8 us  [body(): lax.all_to_all(rows_grad, 'expert', split_axis=0, concat_axis=0, tiled=True)]
  transfers between devices with their start and end apart: 9 -> 10, of which waited for: 5 -> 7; matrix products, arithmetic and copies ran while one was open for 12% -> 10% of each run, Pallas kernels for 0% -> 0%
where the time goes in v1:
time: 953 us; the launch traced here: 942 us
  waiting for transfers between devices  468 us (49%)
  blocking collectives  135 us (14%)
  local copies, waits for them, and re-layouts  121 us (13%)
  matrix products  121 us (13%)
  other arithmetic  58.1 us (6%)
  starting transfers between devices  24.4 us (3%)
  between operations  14.6 us (2%)
    psum x1, waiting for transfers between devices, body(): lax.psum((ln_attn_grad, kv_weight_grad, router_grad, in_weight_grad, out_...  179 us
    all_gather x1, blocking collectives, body(): lax.all_gather(sentence, 'expert', axis=0, tiled=True)  91.3 us
    psum x1, waiting for transfers between devices, body(): lax.psum(lax.psum((ln_attn_grad, kv_weight_grad, router_grad, in_weight_g...  88.3 us
    all_to_all x1, waiting for transfers between devices, body(): lax.all_to_all(route_dispatch, 'expert', split_axis=0, concat_axis=0, til...  70 us
    all_to_all x1, waiting for transfers between devices, body(): lax.all_to_all(results, 'expert', split_axis=0, concat_axis=0, tiled=True)  66.7 us
    dot_general x24, matrix products, product_nt(): lax.dot_general(left, right, (((1,), (1,)), ((), ())), preferred_element_...  43.2 us
    dot_general x20, matrix products, product(): return jnp.dot(left, right, preferred_element_type=jnp.float32)  40.2 us
    dot_general x20, matrix products, product_tn(): lax.dot_general(left, right, (((0,), (0,)), ((), ())), preferred_element_...  37.9 us
  transfers between devices with their start and end apart: 10, of which 7 were waited for; matrix products, arithmetic and copies ran while one was open for 10% of the time, Pallas kernels for 0%

profile of v1, /device:TPU:0, one launch (start us, length us, event | category | flops | bytes accessed | tf_op | source)
XLA Modules:
  0.0 942.1 jit_solution(14380365934967802000)
XLA Ops:
  19.5 8.6 scatter_custom_fusion
  28.2 6.3 all-to-all-start
  44.1 12.1 %scatter_custom_fusion.1 = bf16[3072,512]{1,0:T(8,128)(2,1)} fusion(s32[2048]{0:T(1024)S(1)} %bitcast.204, bf16[2048,512]{1,0:T(8,128)(2,1)} %reshape.339, bf16[]{:T(256)} %constant.98.clone.1), kind=kCustom, calls=%fused_computation.115 | custom fusion | bytes 3146240 | tf_op jit(solution)/shard_map/scatter | solution.py:143
  56.1 5.2 all-to-all-start.1
  62.6 91.3 %all-gather = s32[1,4096]{1,0:T(1,128)S(1)} all-gather(s32[1,1024]{1,0:T(1,128)S(1)} %copy-done.38), channel_id=2, replica_groups=mesh['dp'=4,'expert'=4,'tok'=2] {'expert'}, dimensions={1}, use_global_device_ids=true | all-gather | bytes 20480 | tf_op jit(solution)/shard_map/all_gather | solution.py:158
  157.8 41.3 %while.32 = (s32[]{:T(128)}, bf16[4,768,512]{2,1,0:T(8,128)(2,1)}, bf16[4,768,64]{1,2,0:T(8,128)(2,1)}, bf16[4,768,64]{1,2,0:T(8,128)(2,1)}, f32[4,768]{1,0:T(4,...) while((s32[]{:T(128)}, bf16[4,768,512]{2,1,0:T(8,128)(2,1)}, ...), condition=%wide.region_13.14_spmd, body=%wide.region_10.13_spmd.sunk | while | flops 314277120 | bytes 12918941 | solution.py:169
  199.1 4.8 all-to-all-start.2
  205.0 66.7 %all-to-all-done.2 = bf16[4,768,512]{2,1,0:T(8,128)(2,1)} async-done(((bf16[4,768,512]{2,1,0:T(8,128)(2,1)}), bf16[4,768,512]{2,1,0:T(8,128)(2,1)}, u32[]{:S(2)}, u32[]{:S(2)}) %all-to-all-start.2) | async-done | bytes 3145760 | tf_op jit(solution)/shard_map/all_to_all | solution.py:172
  271.6 11.6 %gather_fusion = bf16[2048,512]{1,0:T(8,128)(2,1)} fusion(bf16[3072,512]{1,0:T(8,128)(2,1)} %bitcast.25, s32[2048]{0:T(1024)S(1)} %broadcast_clamp_fusion), kind=kCustom, calls=%fused_computation | custom fusion | bytes 4202496 | tf_op jit(solution)/shard_map/gather | solution.py:174
  283.2 5.4 reshape.309
  288.6 7.7 multiply_reduce_fusion.2
  297.1 4.7 multiply_convert_fusion.1
  301.8 5.0 fusion.47
  316.2 6.2 mul.257
  322.5 13.1 %scatter_custom_fusion.2 = bf16[3072,512]{1,0:T(8,128)(2,1)} fusion(s32[2048]{0:T(1024)S(1)} %bitcast.206, f32[2048,512]{1,0:T(8,128)} %mul.257, f32[2048]{0:T(1024)S(1)} %div.59, bf16[]{:T(256)} %constant.98.clone.1), kind=kCustom, calls=%fused_computation.102 | custom fusion | flops 2097152 | bytes 7348226 | tf_op jit(solution)/shard_map/scatter | solution.py:204
  339.4 70.0 %all-to-all-done.3 = bf16[4,768,512]{2,1,0:T(8,128)(2,1)S(1)} async-done(((bf16[4,768,512]{2,1,0:T(8,128)(2,1)}), bf16[4,768,512]{2,1,0:T(8,128)(2,1)S(1)}, u32[]{:S(2)}, u32[]{:S(2)}) %all-to-all-start.3) | async-done | bytes 3145760 | tf_op jit(solution)/shard_map/all_to_all | solution.py:207
  411.4 68.3 %while.33 = (s32[]{:T(128)}, bf16[4,768,512]{2,1,0:T(8,128)(2,1)}, bf16[4,1024,128]{2,1,0:T(8,128)(2,1)}, f32[4,512,64]{1,2,0:T(8,128)}, f32[4,64,512]{2,1,0:T(8...) while((s32[]{:T(128)}, bf16[4,768,512]{2,1,0:T(8,128)(2,1)}, ...), condition=%wide.region_22.23_spmd, body=%wide.region_20.22_spmd.sunk | while | flops 713702656 | bytes 31267520 | solution.py:224
  480.1 7.0 fusion.84
  491.8 14.3 %reduce-scatter.2.cloned.1.call-done = bf16[1024,128]{1,0:T(8,128)(2,1)} async-done(((bf16[4096,128]{1,0:T(8,128)(2,1)}), bf16[1024,128]{1,0:T(8,128)(2,1)}) %reduce-scatter.2.cloned.1.call-update) | async-done | bytes 262160 | tf_op jit(solution)/shard_map/reduce_scatter | solution.py:238
  510.6 178.7 %all-reduce.9.cloned.1.call-done = (f32[512,128]{1,0:T(8,128)}, f32[512,2048]{1,0:T(8,128)}, f32[2048,512]{1,0:T(8,128)}) async-done(((f32[512,128]{1,0:T(8,128)}, f32[512,2048]{1,0:T(8,128)}, f32[2048,512]{1,0:T(8,128)}), (f32[512,128]{1,0:T(8,128)}, f32[512,2048]{1,0:T(8,128)}, f32[2048,512]{1,0:T(8,128)})) %all-reduce.9.cloned.1.call-update) | async-done | bytes 8650768 | tf_op jit(solution)/shard_map/psum | solution.py:264
  693.2 5.9 multiply_reduce_fusion.1
  702.5 6.8 add_convert_fusion
  709.3 37.0 %all-reduce.13.cloned.1.call-done = (bf16[1,512,64]{1,2,0:T(8,128)(2,1)}, bf16[1,64,512]{2,1,0:T(8,128)(2,1)}) async-done(((bf16[1,512,64]{1,2,0:T(8,128)(2,1)}, bf16[1,64,512]{2,1,0:T(8,128)(2,1)}), (bf16[1,512,64]{1,2,0:T(8,128)(2,1)}, bf16[1,64,512]{2,1,0:T(8,128)(2,1)})) %all-reduce.13.cloned.1.call-update) | async-done | bytes 131088 | tf_op jit(solution)/shard_map/psum | solution.py:247
  751.1 12.8 %all-to-all-done.4 = bf16[4,768,512]{2,1,0:T(8,128)(2,1)S(1)} async-done(((bf16[4,768,512]{2,1,0:T(8,128)(2,1)}), bf16[4,768,512]{2,1,0:T(8,128)(2,1)S(1)}, u32[]{:S(2)}, u32[]{:S(2)}) %all-to-all-start.4) | async-done | bytes 3145760 | tf_op jit(solution)/shard_map/all_to_all | solution.py:237
  764.0 9.2 gather_fusion.1
  773.2 5.6 reshape.310
  778.8 8.6 reduce_sum.214
  787.5 4.7 fusion.60
  792.2 26.2 %all-reduce = (f32[512]{0:T(512)S(1)}, f32[512,4]{0,1:T(4,128)S(1)}, f32[512]{0:T(512)S(1)}) all-reduce(f32[512]{0:T(512)S(1)} %get-tuple-element.235, f32[512,4]{0,1:T(4,128)S(1)} %copy-done.31, f32[512]{0:T(512)S(1)} %copy-done.39), channel_id=1, replica_groups=mesh['dp'=4,'expert'=4,'tok'=2] {'expert','tok'}, use_global_device_ids=true, to_apply=%region_31.32 | all-reduce | flops 3072 | bytes 24576 | tf_op jit(solution)/shard_map/psum | solution.py:264
  818.4 17.2 %all-reduce.2 = (f32[512]{0:T(512)}, f32[512,4]{0,1:T(4,128)}, f32[512]{0:T(512)}) all-reduce(f32[512]{0:T(512)S(1)} %get-tuple-element.291, f32[512,4]{0,1:T(4,128)S(1)} %get-tuple-element.292, f32[512]{0:T(512)S(1)} %get-tuple-element.293), channel_id=1, replica_groups=mesh['dp'=4,'expert'=4,'tok'=2] {'dp'}, use_global_device_ids=true, to_apply=%region_32.33 | all-reduce | flops 3072 | bytes 24576 | tf_op jit(solution)/shard_map/psum | solution.py:263
  838.6 88.3 %all-reduce.11.cloned.1.call-done = (f32[512,128]{1,0:T(8,128)}, f32[512,2048]{1,0:T(8,128)}, f32[2048,512]{1,0:T(8,128)}) async-done(((f32[512,128]{1,0:T(8,128)}, f32[512,2048]{1,0:T(8,128)}, f32[2048,512]{1,0:T(8,128)}), (f32[512,128]{1,0:T(8,128)}, f32[512,2048]{1,0:T(8,128)}, f32[2048,512]{1,0:T(8,128)})) %all-reduce.11.cloned.1.call-update) | async-done | bytes 8650768 | tf_op jit(solution)/shard_map/psum | solution.py:263
  928.5 4.8 copy.169
  (278 shorter events, 181.2 us)
Async XLA Ops:
  7.2 289.9 %copy-start = (bf16[512,2048]{1,0:T(8,128)(2,1)S(1)}, bf16[512,2048]{1,0:T(8,128)(2,1)}, u32[]{:S(2)}) copy-start(bf16[512,2048]{1,0:T(8,128)(2,1)} %param.26) | copy-start | bytes 6291460
  7.2 27.3 %copy-start.6 = (bf16[1024,512]{1,0:T(8,128)(2,1)S(1)}, bf16[1024,512]{1,0:T(8,128)(2,1)}, u32[]{:S(2)}) copy-start(bf16[1024,512]{1,0:T(8,128)(2,1)} %param.16) | copy-start | bytes 3145732
  7.2 28.7 %copy-start.32 = (f32[512]{0:T(512)S(1)}, f32[512]{0:T(512)}, u32[]{:S(2)}) copy-start(f32[512]{0:T(512)} %param.20) | copy-start | bytes 6148
  28.2 28.0 %all-to-all-start = ((s32[4,1,768]{2,1,0:T(1,128)}), s32[4,1,768]{2,1,0:T(1,128)S(1)}, u32[]{:S(2)}, u32[]{:S(2)}) async-start(s32[4,1,768]{2,1,0:T(1,128)} %bitcast.20), calls=%async_computation | async-start | bytes 24576 | tf_op jit(solution)/shard_map/all_to_all | solution.py:154
  37.5 166.4 %copy-start.4 = (bf16[1024,512]{1,0:T(8,128)(2,1)}, bf16[1024,512]{1,0:T(8,128)(2,1)S(1)}, u32[]{:S(2)}) copy-start(bf16[1024,512]{1,0:T(8,128)(2,1)S(1)} %fusion.54) | copy-start | bytes 3145732
  56.1 99.0 %copy-start.28 = (bf16[1,512,64]{1,2,0:T(8,128)(2,1)S(1)}, bf16[1,512,64]{1,2,0:T(8,128)(2,1)}, u32[]{:S(2)}) copy-start(bf16[1,512,64]{1,2,0:T(8,128)(2,1)} %param.23) | copy-start | bytes 196612
  56.1 99.7 %all-to-all-start.1 = ((bf16[4,768,512]{2,1,0:T(8,128)(2,1)}), bf16[4,768,512]{2,1,0:T(8,128)(2,1)}, u32[]{:S(2)}, u32[]{:S(2)}) async-start(bf16[4,768,512]{2,1,0:T(8,128)(2,1)} %bitcast.192), calls=%async_computation.1 | async-start | bytes 6291456 | tf_op jit(solution)/shard_map/all_to_all | solution.py:153
  61.4 94.5 %all-gather.3.cloned.1.call-start = ((), (), s32[]{:S(2)}) async-start(), calls=%async_computation.6 | async-start | bytes 1310720 | tf_op jit(solution)/shard_map/all_gather | solution.py:157
  199.1 72.5 %all-to-all-start.2 = ((bf16[4,768,512]{2,1,0:T(8,128)(2,1)}), bf16[4,768,512]{2,1,0:T(8,128)(2,1)}, u32[]{:S(2)}, u32[]{:S(2)}) async-start(bf16[4,768,512]{2,1,0:T(8,128)(2,1)} %get-tuple-element.150), calls=%async_computation.2 | async-start | bytes 6291456 | tf_op jit(solution)/shard_map/all_to_all | solution.py:172
  204.4 78.8 %copy-start.29 = (f32[1024]{0:T(1024)}, f32[1024]{0:T(1024)S(1)}, u32[]{:S(2)}) copy-start(f32[1024]{0:T(1024)S(1)} %fusion.74) | copy-start | bytes 12292
  204.9 78.3 %copy-start.24 = (s32[2048]{0:T(1024)}, s32[2048]{0:T(1024)S(1)}, u32[]{:S(2)}) copy-start(s32[2048]{0:T(1024)S(1)} %broadcast_clamp_fusion) | copy-start | bytes 24580
  288.6 7.7 copy-start.7
  296.6 13.7 %copy-start.2 = (f32[1024,512]{1,0:T(8,128)}, f32[1024,512]{1,0:T(8,128)S(1)}, u32[]{:S(2)}) copy-start(f32[1024,512]{1,0:T(8,128)S(1)} %get-tuple-element.306) | copy-start | bytes 6291460
  335.6 73.8 %all-to-all-start.3 = ((bf16[4,768,512]{2,1,0:T(8,128)(2,1)}), bf16[4,768,512]{2,1,0:T(8,128)(2,1)S(1)}, u32[]{:S(2)}, u32[]{:S(2)}) async-start(bf16[4,768,512]{2,1,0:T(8,128)(2,1)} %bitcast.193), calls=%async_computation.3 | async-start | bytes 6291456 | tf_op jit(solution)/shard_map/all_to_all | solution.py:207
  339.3 166.7 %reduce-scatter.2.cloned.1.call-start = ((), (), s32[]{:S(2)}) async-start(), calls=%async_computation.7 | async-start | bytes 1310720 | tf_op jit(solution)/shard_map/reduce_scatter | solution.py:238
  479.6 209.7 %all-reduce.9.cloned.1.call-start = ((), (), s32[]{:S(2)}) async-start(), calls=%async_computation.8 | async-start | bytes 17301504 | tf_op jit(solution)/shard_map/psum | solution.py:264
  480.1 7.0 copy-start.3
  487.1 18.9 %copy-start.5 = (bf16[1024,512]{1,0:T(8,128)(2,1)S(1)}, bf16[1024,512]{1,0:T(8,128)(2,1)}, u32[]{:S(2)}) copy-start(bf16[1024,512]{1,0:T(8,128)(2,1)} %copy-done.4) | copy-start | bytes 3145732
  508.2 238.1 %all-reduce.13.cloned.1.call-start = ((), (), s32[]{:S(2)}) async-start(), calls=%async_computation.10 | async-start | bytes 262144 | tf_op jit(solution)/shard_map/psum | solution.py:247
  510.6 416.3 %all-reduce.11.cloned.1.call-start = ((), (), s32[]{:S(2)}) async-start(), calls=%async_computation.9 | async-start | bytes 17301504 | tf_op jit(solution)/shard_map/psum | solution.py:263
  689.4 74.6 %all-to-all-start.4 = ((bf16[4,768,512]{2,1,0:T(8,128)(2,1)}), bf16[4,768,512]{2,1,0:T(8,128)(2,1)S(1)}, u32[]{:S(2)}, u32[]{:S(2)}) async-start(bf16[4,768,512]{2,1,0:T(8,128)(2,1)} %get-tuple-element.155), calls=%async_computation.5 | async-start | bytes 6291456 | tf_op jit(solution)/shard_map/all_to_all | solution.py:237
  693.2 7.2 copy-start.30
  693.2 7.2 copy-start.21
  702.5 46.8 %copy-start.14 = (bf16[1024,128]{1,0:T(8,128)(2,1)S(1)}, bf16[1024,128]{1,0:T(8,128)(2,1)}, u32[]{:S(2)}) copy-start(bf16[1024,128]{1,0:T(8,128)(2,1)} %reduce-scatter.2.cloned.1.call-done) | copy-start | bytes 786436
  702.5 46.8 %copy-start.19 = (bf16[512,128]{1,0:T(8,128)(2,1)S(1)}, bf16[512,128]{1,0:T(8,128)(2,1)}, u32[]{:S(2)}) copy-start(bf16[512,128]{1,0:T(8,128)(2,1)} %param.21) | copy-start | bytes 393220
  702.5 61.5 %copy-start.25 = (s32[2048]{0:T(1024)S(1)}, s32[2048]{0:T(1024)}, u32[]{:S(2)}) copy-start(s32[2048]{0:T(1024)} %copy-done.24) | copy-start | bytes 24580
  778.8 8.6 copy-start.8
  778.8 8.6 copy-start.23
  778.8 8.6 copy-start.27
  778.8 8.6 copy-start.33
  778.8 8.6 copy-start.37
  787.4 48.1 %copy-start.10 = (f32[1024,512]{1,0:T(8,128)S(1)}, f32[1024,512]{1,0:T(8,128)}, u32[]{:S(2)}) copy-start(f32[1024,512]{1,0:T(8,128)} %copy-done.9) | copy-start | bytes 6291460
  (19 other events, 75.8 us)
Sparse Core Ops, SparseCore 0:
  64.3 43.4 all-gather.2
  479.8 26.2 reduce-scatter.1
  509.4 179.8 all-reduce.8
  693.1 53.1 all-reduce.12
  750.1 176.6 all-reduce.10
